TPU v7x, 32 devices: a whole 2x2x4 slice. The times are simulated.
32 devices in a mesh: clip: 8 (over y, x, core), cap: 4 (over z).
Axes of the slice: x: 2, y: 2, z: 4, core: 2. Of those that a mesh axis runs over, the one named last changes fastest.
Arguments:
- teacher_audio: bfloat16 [6144, 512], P(('clip', 'cap')), may hold values from -2 to 2
- teacher_text: bfloat16 [6144, 512], P(('cap', 'clip')), may hold values from -2 to 2
- student_audio: bfloat16 [6144, 512], P(('clip', 'cap')), may hold values from -2 to 2
- student_text: bfloat16 [6144, 512], P(('cap', 'clip')), may hold values from -2 to 2
Outputs:
- audio_grad: float32 [6144, 512], P(('clip', 'cap'))
- text_grad: float32 [6144, 512], P(('cap', 'clip'))
All inputs are finite; a program needn't handle non-finite values.
Results may differ from a plain program's by a relative error of at most 0.0026.
Values may be sent and summed in bfloat16 or wider, within the bound.
A program may use at most 128 MiB of HBM per device.

v0:
```python
import jax
import jax.numpy as jnp
from jax import lax
from jax.sharding import PartitionSpec as P

ITERS = 3


def contract_rows(left_mat, right_mat):
    return lax.dot_general(
        left_mat, right_mat, (((1,), (1,)), ((), ())), preferred_element_type=jnp.float32
    )


def contract_first(left_mat, right_mat):
    return lax.dot_general(
        left_mat, right_mat, (((0,), (0,)), ((), ())), preferred_element_type=jnp.float32
    )


def body(teacher_audio, teacher_text, student_audio, student_text):
    audio_teacher, audio_student = (
        lax.all_gather(teacher_audio, "cap", axis=0, tiled=True),
        lax.all_gather(student_audio, "cap", axis=0, tiled=True),
    )
    text_teacher, text_student = (
        lax.all_gather(teacher_text, "clip", axis=0, tiled=True),
        lax.all_gather(student_text, "clip", axis=0, tiled=True),
    )
    teacher_logits = 10.0 * contract_rows(audio_teacher, text_teacher)
    student_logits = 10.0 * contract_rows(audio_student, text_student)
    teacher_max, student_max = lax.pmax(
        (jnp.max(teacher_logits, axis=1), jnp.max(student_logits, axis=1)), "cap"
    )
    student_exp = jnp.exp(student_logits - student_max[:, None])
    student_total = lax.psum(jnp.sum(student_exp, axis=1), "cap")
    kernel = jnp.exp(teacher_logits - teacher_max[:, None])
    weights_row = jnp.ones((kernel.shape[0],), jnp.float32)
    column_scale = jnp.ones((kernel.shape[1],), jnp.float32)
    for sweep_index in range(ITERS):
        column = lax.psum(jnp.dot(weights_row, kernel, precision=lax.Precision.HIGHEST), "clip")
        column_scale = 1.0 / column
        row_total = lax.psum(jnp.dot(kernel, column_scale, precision=lax.Precision.HIGHEST), "cap")
        weights_row = 1.0 / row_total
    target = weights_row[:, None] * kernel * column_scale[None, :]
    student_prob = student_exp / student_total[:, None]
    residual = (student_prob - target).astype(jnp.bfloat16)
    audio_grad = lax.psum_scatter(
        10.0 * jnp.dot(residual, text_student, preferred_element_type=jnp.float32),
        "cap",
        scatter_dimension=0,
        tiled=True,
    )
    text_grad = lax.psum_scatter(
        10.0 * contract_first(residual, audio_student), "clip", scatter_dimension=0, tiled=True
    )
    return (audio_grad, text_grad)


def solution(mesh):
    placed = (
        P(("clip", "cap"), None),
        P(("cap", "clip"), None),
        P(("clip", "cap"), None),
        P(("cap", "clip"), None),
    )
    return jax.shard_map(
        body,
        mesh=mesh,
        in_specs=placed,
        out_specs=(P(("clip", "cap"), None), P(("cap", "clip"), None)),
        check_vma=False,
    )
```

profile of v0, /device:TPU:0, one launch (start us, length us, event | category | flops | bytes accessed | tf_op | source)
XLA Modules:
  0.0 283.5 jit_solution(820184726141326755)
XLA Ops:
  7.2 0.0 all-gather.5.cloned.1.call-start
  7.2 0.7 all-gather.5.cloned.1.call-update
  7.9 0.0 all-gather.3.cloned.1.call-start
  7.9 0.7 all-gather.3.cloned.1.call-update
  8.6 0.0 reduce-scatter.3.cloned.1.call-start
  8.7 21.5 %all_gather.12 = bf16[768,512]{1,0:T(8,128)(2,1)S(1)} all-gather(bf16[192,512]{1,0:T(8,128)(2,1)} %param.6), channel_id=1, replica_groups=mesh['clip'=8,'cap'=4] {'cap'}, dimensions={0}, use_global_device_ids=true | all-gather | bytes 983040 | tf_op jit(solution)/shard_map/all_gather | solution.py:24
  30.2 17.9 %all_gather.14 = bf16[768,512]{1,0:T(8,128)(2,1)S(1)} all-gather(bf16[192,512]{1,0:T(8,128)(2,1)} %param.4), channel_id=1, replica_groups=mesh['clip'=8,'cap'=4] {'cap'}, dimensions={0}, use_global_device_ids=true | all-gather | bytes 983040 | tf_op jit(solution)/shard_map/all_gather | solution.py:23
  48.1 0.0 all-gather.5.cloned.1.call-done
  48.1 5.0 %multiply_reduce_fusion = (f32[768]{0:T(1024)S(1)}, f32[768,1536]{1,0:T(8,128)}) fusion(bf16[768,512]{1,0:T(8,128)(2,1)S(1)} %all_gather.14, bf16[1536,512]{1,0:T(8,128)(2,1)} %all-gather.5.cloned.1.call-done), kind=kOutput, calls=%fused_computation.3 | convolution fusion | flops 1210318080 | bytes 7080960 | tf_op jit(solution)/shard_map/dot_general | solution.py:10
  53.1 12.6 %all-gather.3.cloned.1.call-done = bf16[1536,512]{1,0:T(8,128)(2,1)} async-done(((bf16[192,512]{1,0:T(8,128)(2,1)}), bf16[1536,512]{1,0:T(8,128)(2,1)}) %all-gather.3.cloned.1.call-update) | async-done | bytes 1572880 | tf_op jit(solution)/shard_map/all_gather | solution.py:28
  65.7 5.0 %multiply_reduce_fusion.1 = (f32[768]{0:T(1024)S(1)}, f32[768,1536]{1,0:T(8,128)}) fusion(bf16[768,512]{1,0:T(8,128)(2,1)S(1)} %all_gather.12, bf16[1536,512]{1,0:T(8,128)(2,1)} %all-gather.3.cloned.1.call-done), kind=kOutput, calls=%fused_computation.4 | convolution fusion | flops 1210318080 | bytes 7080960 | tf_op jit(solution)/shard_map/dot_general | solution.py:10
  70.7 11.8 %all-reduce.1 = (f32[768]{0:T(1024)S(1)}, f32[768]{0:T(1024)S(1)}) all-reduce(f32[768]{0:T(1024)S(1)} %get-tuple-element.6, f32[768]{0:T(1024)S(1)} %get-tuple-element.8), channel_id=1, replica_groups=mesh['clip'=8,'cap'=4] {'cap'}, use_global_device_ids=true, to_apply=%region_5.0 | all-reduce | flops 1536 | bytes 12288 | tf_op jit(solution)/shard_map/pmax | solution.py:32
  82.5 5.3 %convolution_reduce_fusion.2 = f32[1536]{0:T(1024)S(1)} fusion(f32[768,1536]{1,0:T(8,128)} %get-tuple-element.7, f32[768]{0:T(1024)S(1)} %get-tuple-element.4), kind=kOutput, calls=%fused_computation.10 | convolution fusion | flops 16515072 | bytes 4727808 | tf_op jit(solution)/shard_map/dot_general | solution.py:41
  87.8 12.1 %psum.50 = f32[1536]{0:T(1024)S(1)} all-reduce(f32[1536]{0:T(1024)S(1)} %convolution_reduce_fusion.2), channel_id=1, replica_groups=mesh['clip'=8,'cap'=4] {'clip'}, use_global_device_ids=true, to_apply=%region_6.0 | all-reduce | flops 1536 | bytes 12288 | tf_op jit(solution)/shard_map/psum | solution.py:41
  99.9 6.9 %convolution_reduce_fusion.5 = f32[768]{0:T(1024)S(1)} fusion(f32[1536,1]{0,1:T(1,128)S(1)} %reshape.11, f32[768,1536]{1,0:T(8,128)} %get-tuple-element.7, f32[768]{0:T(1024)S(1)} %get-tuple-element.4), kind=kOutput, calls=%fused_computation.13 | convolution fusion | flops 16515072 | bytes 4730880 | tf_op jit(solution)/shard_map/dot_general | solution.py:43
  106.8 8.4 %psum.51 = f32[768]{0:T(1024)S(1)} all-reduce(f32[768]{0:T(1024)S(1)} %convolution_reduce_fusion.5), channel_id=1, replica_groups=mesh['clip'=8,'cap'=4] {'cap'}, use_global_device_ids=true, to_apply=%region_7.0 | all-reduce | flops 768 | bytes 6144 | tf_op jit(solution)/shard_map/psum | solution.py:43
  115.2 5.3 %convolution_reduce_fusion.1 = f32[1536]{0:T(1024)S(1)} fusion(f32[768,1]{0,1:T(1,128)S(1)} %reshape.13, f32[768,1536]{1,0:T(8,128)} %get-tuple-element.7, f32[768]{0:T(1024)S(1)} %get-tuple-element.4), kind=kOutput, calls=%fused_computation.9 | convolution fusion | flops 16515072 | bytes 4730880 | tf_op jit(solution)/shard_map/dot_general | solution.py:41
  120.5 12.0 %psum.52 = f32[1536]{0:T(1024)S(1)} all-reduce(f32[1536]{0:T(1024)S(1)} %convolution_reduce_fusion.1), channel_id=1, replica_groups=mesh['clip'=8,'cap'=4] {'clip'}, use_global_device_ids=true, to_apply=%region_8.0 | all-reduce | flops 1536 | bytes 12288 | tf_op jit(solution)/shard_map/psum | solution.py:41
  132.6 6.9 %convolution_reduce_fusion.4 = f32[768]{0:T(1024)S(1)} fusion(f32[1536,1]{0,1:T(1,128)S(1)} %reshape.15, f32[768,1536]{1,0:T(8,128)} %get-tuple-element.7, f32[768]{0:T(1024)S(1)} %get-tuple-element.4), kind=kOutput, calls=%fused_computation.12 | convolution fusion | flops 16515072 | bytes 4730880 | tf_op jit(solution)/shard_map/dot_general | solution.py:43
  139.5 10.4 %psum.53 = f32[768]{0:T(1024)S(1)} all-reduce(f32[768]{0:T(1024)S(1)} %convolution_reduce_fusion.4), channel_id=1, replica_groups=mesh['clip'=8,'cap'=4] {'cap'}, use_global_device_ids=true, to_apply=%region_9.0 | all-reduce | flops 768 | bytes 6144 | tf_op jit(solution)/shard_map/psum | solution.py:43
  149.9 5.3 %convolution_reduce_fusion = f32[1536]{0:T(1024)S(1)} fusion(f32[768,1]{0,1:T(1,128)S(1)} %reshape.17, f32[768,1536]{1,0:T(8,128)} %get-tuple-element.7, f32[768]{0:T(1024)S(1)} %get-tuple-element.4), kind=kOutput, calls=%fused_computation.8 | convolution fusion | flops 16515072 | bytes 4730880 | tf_op jit(solution)/shard_map/dot_general | solution.py:41
  155.2 12.3 %psum.54 = f32[1536]{0:T(1024)S(1)} all-reduce(f32[1536]{0:T(1024)S(1)} %convolution_reduce_fusion), channel_id=1, replica_groups=mesh['clip'=8,'cap'=4] {'clip'}, use_global_device_ids=true, to_apply=%region_10.0 | all-reduce | flops 1536 | bytes 12288 | tf_op jit(solution)/shard_map/psum | solution.py:41
  167.5 6.9 %convolution_reduce_fusion.3 = f32[768]{0:T(1024)S(1)} fusion(f32[1536,1]{0,1:T(1,128)S(1)} %reshape.19, f32[768,1536]{1,0:T(8,128)} %get-tuple-element.7, f32[768]{0:T(1024)S(1)} %get-tuple-element.4), kind=kOutput, calls=%fused_computation.11 | convolution fusion | flops 16515072 | bytes 4730880 | tf_op jit(solution)/shard_map/dot_general | solution.py:43
  174.4 3.2 %fusion = f32[768]{0:T(1024)S(1)} fusion(f32[768,1536]{1,0:T(8,128)} %get-tuple-element.9, f32[768]{0:T(1024)S(1)} %get-tuple-element.5), kind=kLoop, calls=%fused_computation.5 | loop fusion | flops 3538176 | bytes 4724736 | tf_op jit(solution)/shard_map/reduce_sum | solution.py:36
  177.7 8.5 %all-reduce = (f32[768]{0:T(1024)S(1)}, f32[768]{0:T(1024)S(1)}) all-reduce(f32[768]{0:T(1024)S(1)} %convolution_reduce_fusion.3, f32[768]{0:T(1024)S(1)} %fusion), channel_id=1, replica_groups=mesh['clip'=8,'cap'=4] {'cap'}, use_global_device_ids=true, to_apply=%region_11.0 | all-reduce | flops 1536 | bytes 12288 | tf_op jit(solution)/shard_map/psum | solution.py:43
  186.2 0.0 copy-start
  186.2 4.9 %subtract_convert_fusion = bf16[768,1536]{1,0:T(8,128)(2,1)S(1)} fusion(f32[768,1536]{1,0:T(8,128)} %get-tuple-element.9, f32[1536]{0:T(1024)S(1)} %broadcast_divide_fusion, f32[768]{0:T(1024)S(1)} %broadcast_divide_fusion.5, f32[768]{0:T(1024)S(1)} %get-tuple-element.3, f32[768]{0:T(1024)S(1)} %get-tuple-element.5, f32[768]{0:T(1024)S(1)} %get-tuple-element.4, ...), kind=kLoop, calls=%fused_computation | loop fusion | flops 10616832 | bytes 11814912 | tf_op jit(solution)/shard_map/convert_element_type | solution.py:47
  191.2 0.0 copy-done
  191.2 2.5 convolution_multiply_fusion.1
  193.7 0.0 reduce-scatter.3.cloned.1.call-update
  193.7 0.0 reduce-scatter.5.cloned.1.call-start
  193.8 3.1 %convolution_multiply_fusion = f32[1536,512]{1,0:T(8,128)} fusion(bf16[768,1536]{1,0:T(8,128)(2,1)S(1)} %subtract_convert_fusion, bf16[768,512]{1,0:T(8,128)(2,1)S(1)} %all_gather.12), kind=kOutput, calls=%fused_computation.6 | convolution fusion | flops 1208745984 | bytes 6291456 | tf_op jit(solution)/shard_map/dot_general | solution.py:16
  196.9 0.0 reduce-scatter.5.cloned.1.call-update
  196.9 31.3 %reduce-scatter.3.cloned.1.call-done = f32[192,512]{1,0:T(8,128)} async-done(((f32[768,512]{1,0:T(8,128)}), f32[192,512]{1,0:T(8,128)}) %reduce-scatter.3.cloned.1.call-update) | async-done | bytes 393232 | tf_op jit(solution)/shard_map/reduce_scatter | solution.py:48
  228.2 48.7 %reduce-scatter.5.cloned.1.call-done = f32[192,512]{1,0:T(8,128)} async-done(((f32[1536,512]{1,0:T(8,128)}), f32[192,512]{1,0:T(8,128)}) %reduce-scatter.5.cloned.1.call-update) | async-done | bytes 393232 | tf_op jit(solution)/shard_map/reduce_scatter | solution.py:54
  (11 shorter events, 0.1 us)
Async XLA Ops:
  7.2 41.0 %all-gather.5.cloned.1.call-start = ((), (), s32[]{:S(2)}) async-start(), calls=%async_computation.3 | async-start | bytes 1769472 | tf_op jit(solution)/shard_map/all_gather | solution.py:27
  7.9 57.8 %all-gather.3.cloned.1.call-start = ((), (), s32[]{:S(2)}) async-start(), calls=%async_computation.2 | async-start | bytes 1769472 | tf_op jit(solution)/shard_map/all_gather | solution.py:28
  8.6 219.5 %reduce-scatter.3.cloned.1.call-start = ((), (), s32[]{:S(2)}) async-start(), calls=%async_computation.4 | async-start | bytes 1966080 | tf_op jit(solution)/shard_map/reduce_scatter | solution.py:48
  186.2 5.0 %copy-start = (bf16[1536,512]{1,0:T(8,128)(2,1)S(1)}, bf16[1536,512]{1,0:T(8,128)(2,1)}, u32[]{:S(2)}) copy-start(bf16[1536,512]{1,0:T(8,128)(2,1)} %all-gather.3.cloned.1.call-done) | copy-start | bytes 4718596
  193.7 83.2 %reduce-scatter.5.cloned.1.call-start = ((), (), s32[]{:S(2)}) async-start(), calls=%async_computation.5 | async-start | bytes 3538944 | tf_op jit(solution)/shard_map/reduce_scatter | solution.py:54
Sparse Core Ops, SparseCore 0:
  9.8 28.2 all-gather.4
  40.1 25.5 all-gather.2
  193.9 34.2 reduce-scatter.2
  232.0 44.8 reduce-scatter.4
where the time goes:
time: 284 us; the launch traced here: 283 us
  blocking collectives  115 us (40%)
  waiting for transfers between devices  94 us (33%)
  matrix products  52.1 us (18%)
  between operations  13.9 us (5%)
  other arithmetic  8.21 us (3%)
    reduce_scatter x1, waiting for transfers between devices, body(): lax.psum_scatter(10.0 * contract_first(residual, audio_student), 'clip',...  48.7 us
    psum x3, blocking collectives, body(): lax.psum(jnp.dot(weights_row, kernel, precision=lax.Precision.HIGHEST), '...  36.4 us
    reduce_scatter x1, waiting for transfers between devices, body(): lax.psum_scatter(10.0 * jnp.dot(residual, text_student, preferred_element...  31.3 us
    psum x3, blocking collectives, body(): lax.psum(jnp.dot(kernel, column_scale, precision=lax.Precision.HIGHEST),...  27.3 us
    all_gather x1, blocking collectives, body(): lax.all_gather(student_audio, 'cap', axis=0, tiled=True)  21.5 us
    dot_general x3, matrix products, body(): jnp.dot(kernel, column_scale, precision=lax.Precision.HIGHEST)  20.8 us
    all_gather x1, blocking collectives, body(): lax.all_gather(teacher_audio, 'cap', axis=0, tiled=True)  17.9 us
    dot_general x3, matrix products, body(): jnp.dot(weights_row, kernel, precision=lax.Precision.HIGHEST)  15.8 us
  transfers between devices with their start and end apart: 4, of which 3 were waited for; matrix products, arithmetic and copies ran while one was open for 3% of the time, Pallas kernels for 0%

commit v1 on v0

--- a/solution.py
+++ b/solution.py
@@ -38,7 +38,10 @@
     weights_row = jnp.ones((kernel.shape[0],), jnp.float32)
     column_scale = jnp.ones((kernel.shape[1],), jnp.float32)
     for sweep_index in range(ITERS):
-        column = lax.psum(jnp.dot(weights_row, kernel, precision=lax.Precision.HIGHEST), "clip")
+        column = jnp.sum(
+            lax.all_gather(jnp.dot(weights_row, kernel, precision=lax.Precision.HIGHEST), "clip"),
+            axis=0,
+        )
         column_scale = 1.0 / column
         row_total = lax.psum(jnp.dot(kernel, column_scale, precision=lax.Precision.HIGHEST), "cap")
         weights_row = 1.0 / row_total

time: 284 us -> 274 us (0.965)
  blocking collectives: 115 us -> 105 us
    psum x3 -> x0, blocking collectives: 36.4 us -> none  [body(): lax.psum(jnp.dot(weights_row, kernel, precision=lax.Precision.HIGHEST), '...]
    all_gather x0 -> x3, blocking collectives: none -> 26.7 us  [body(): lax.all_gather(jnp.dot(weights_row, kernel, precision=lax.Precision.HIGHE...]
where the time goes in v1:
time: 274 us
  blocking collectives  105 us (38%)
  waiting for transfers between devices  93.8 us (34%)
  matrix products  52.1 us (19%)
  between operations  13.9 us (5%)
  other arithmetic  8.34 us (3%)
    reduce_scatter x1, waiting for transfers between devices, body(): lax.psum_scatter(10.0 * contract_first(residual, audio_student), 'clip',...  48.7 us
    reduce_scatter x1, waiting for transfers between devices, body(): lax.psum_scatter(10.0 * jnp.dot(residual, text_student, preferred_element...  31.1 us
    psum x3, blocking collectives, body(): lax.psum(jnp.dot(kernel, column_scale, precision=lax.Precision.HIGHEST),...  27.3 us
    all_gather x3, blocking collectives, body(): lax.all_gather(jnp.dot(weights_row, kernel, precision=lax.Precision.HIGHE...  26.7 us
    all_gather x1, blocking collectives, body(): lax.all_gather(student_audio, 'cap', axis=0, tiled=True)  21.5 us
    dot_general x3, matrix products, body(): jnp.dot(kernel, column_scale, precision=lax.Precision.HIGHEST)  20.8 us
    all_gather x1, blocking collectives, body(): lax.all_gather(teacher_audio, 'cap', axis=0, tiled=True)  17.9 us
    dot_general x3, matrix products, body(): jnp.dot(weights_row, kernel, precision=lax.Precision.HIGHEST)  15.8 us
  transfers between devices with their start and end apart: 4, of which 3 were waited for; matrix products, arithmetic and copies ran while one was open for 3% of the time, Pallas kernels for 0%

profile of v1, /device:TPU:0, one launch (start us, length us, event | category | flops | bytes accessed | tf_op | source)
XLA Modules:
  0.0 273.6 jit_solution(18262851329858294248)
XLA Ops:
  7.2 0.0 all-gather.11.cloned.1.call-start
  7.2 0.7 all-gather.11.cloned.1.call-update
  7.9 0.0 all-gather.9.cloned.1.call-start
  7.9 0.7 all-gather.9.cloned.1.call-update
  8.6 0.0 reduce-scatter.3.cloned.1.call-start
  8.7 21.5 %all_gather.30 = bf16[768,512]{1,0:T(8,128)(2,1)S(1)} all-gather(bf16[192,512]{1,0:T(8,128)(2,1)} %param.6), channel_id=1, replica_groups=mesh['clip'=8,'cap'=4] {'cap'}, dimensions={0}, use_global_device_ids=true | all-gather | bytes 983040 | tf_op jit(solution)/shard_map/all_gather | solution.py:24
  30.2 17.9 %all_gather.32 = bf16[768,512]{1,0:T(8,128)(2,1)S(1)} all-gather(bf16[192,512]{1,0:T(8,128)(2,1)} %param.4), channel_id=1, replica_groups=mesh['clip'=8,'cap'=4] {'cap'}, dimensions={0}, use_global_device_ids=true | all-gather | bytes 983040 | tf_op jit(solution)/shard_map/all_gather | solution.py:23
  48.1 0.0 all-gather.11.cloned.1.call-done
  48.1 5.0 %multiply_reduce_fusion = (f32[768]{0:T(1024)S(1)}, f32[768,1536]{1,0:T(8,128)}) fusion(bf16[768,512]{1,0:T(8,128)(2,1)S(1)} %all_gather.32, bf16[1536,512]{1,0:T(8,128)(2,1)} %all-gather.11.cloned.1.call-done), kind=kOutput, calls=%fused_computation.3 | convolution fusion | flops 1210318080 | bytes 7080960 | tf_op jit(solution)/shard_map/dot_general | solution.py:10
  53.1 12.6 %all-gather.9.cloned.1.call-done = bf16[1536,512]{1,0:T(8,128)(2,1)} async-done(((bf16[192,512]{1,0:T(8,128)(2,1)}), bf16[1536,512]{1,0:T(8,128)(2,1)}) %all-gather.9.cloned.1.call-update) | async-done | bytes 1572880 | tf_op jit(solution)/shard_map/all_gather | solution.py:28
  65.7 5.0 %multiply_reduce_fusion.1 = (f32[768]{0:T(1024)S(1)}, f32[768,1536]{1,0:T(8,128)}) fusion(bf16[768,512]{1,0:T(8,128)(2,1)S(1)} %all_gather.30, bf16[1536,512]{1,0:T(8,128)(2,1)} %all-gather.9.cloned.1.call-done), kind=kOutput, calls=%fused_computation.4 | convolution fusion | flops 1210318080 | bytes 7080960 | tf_op jit(solution)/shard_map/dot_general | solution.py:10
  70.7 11.8 %all-reduce.1 = (f32[768]{0:T(1024)S(1)}, f32[768]{0:T(1024)S(1)}) all-reduce(f32[768]{0:T(1024)S(1)} %get-tuple-element.6, f32[768]{0:T(1024)S(1)} %get-tuple-element.8), channel_id=1, replica_groups=mesh['clip'=8,'cap'=4] {'cap'}, use_global_device_ids=true, to_apply=%region_5.0 | all-reduce | flops 1536 | bytes 12288 | tf_op jit(solution)/shard_map/pmax | solution.py:32
  82.5 5.3 %convolution_bitcast_fusion.2 = f32[1,1,1536]{2,1,0:T(1,128)S(1)} fusion(f32[768,1536]{1,0:T(8,128)} %get-tuple-element.7, f32[768]{0:T(1024)S(1)} %get-tuple-element.4), kind=kOutput, calls=%fused_computation.9 | convolution fusion | flops 16515072 | bytes 4727808 | tf_op jit(solution)/shard_map/dot_general | solution.py:42
  87.7 9.1 %all-gather.3 = f32[8,1,1536]{2,1,0:T(1,128)S(1)} all-gather(f32[1,1,1536]{2,1,0:T(1,128)S(1)} %convolution_bitcast_fusion.2), channel_id=2, replica_groups=mesh['clip'=8,'cap'=4] {'clip'}, dimensions={0}, use_global_device_ids=true | all-gather | bytes 55296 | tf_op jit(solution)/shard_map/all_gather | solution.py:42
  96.9 6.9 %convolution_reduce_fusion.2 = f32[768]{0:T(1024)S(1)} fusion(f32[1536,1]{0,1:T(1,128)S(1)} %reshape.25, f32[768,1536]{1,0:T(8,128)} %get-tuple-element.7, f32[768]{0:T(1024)S(1)} %get-tuple-element.4), kind=kOutput, calls=%fused_computation.13 | convolution fusion | flops 16515072 | bytes 4730880 | tf_op jit(solution)/shard_map/dot_general | solution.py:46
  103.9 8.4 %psum.29 = f32[768]{0:T(1024)S(1)} all-reduce(f32[768]{0:T(1024)S(1)} %convolution_reduce_fusion.2), channel_id=1, replica_groups=mesh['clip'=8,'cap'=4] {'cap'}, use_global_device_ids=true, to_apply=%region_7.0 | all-reduce | flops 768 | bytes 6144 | tf_op jit(solution)/shard_map/psum | solution.py:46
  112.3 5.3 %convolution_bitcast_fusion.1 = f32[1,1,1536]{2,1,0:T(1,128)S(1)} fusion(f32[768,1]{0,1:T(1,128)S(1)} %reshape.27, f32[768,1536]{1,0:T(8,128)} %get-tuple-element.7, f32[768]{0:T(1024)S(1)} %get-tuple-element.4), kind=kOutput, calls=%fused_computation.8 | convolution fusion | flops 16515072 | bytes 4730880 | tf_op jit(solution)/shard_map/dot_general | solution.py:42
  117.5 8.2 %all-gather.4 = f32[8,1,1536]{2,1,0:T(1,128)S(1)} all-gather(f32[1,1,1536]{2,1,0:T(1,128)S(1)} %convolution_bitcast_fusion.1), channel_id=3, replica_groups=mesh['clip'=8,'cap'=4] {'clip'}, dimensions={0}, use_global_device_ids=true | all-gather | bytes 55296 | tf_op jit(solution)/shard_map/all_gather | solution.py:42
  125.8 6.9 %convolution_reduce_fusion.1 = f32[768]{0:T(1024)S(1)} fusion(f32[1536,1]{0,1:T(1,128)S(1)} %reshape.29, f32[768,1536]{1,0:T(8,128)} %get-tuple-element.7, f32[768]{0:T(1024)S(1)} %get-tuple-element.4), kind=kOutput, calls=%fused_computation.12 | convolution fusion | flops 16515072 | bytes 4730880 | tf_op jit(solution)/shard_map/dot_general | solution.py:46
  132.7 10.4 %psum.30 = f32[768]{0:T(1024)S(1)} all-reduce(f32[768]{0:T(1024)S(1)} %convolution_reduce_fusion.1), channel_id=1, replica_groups=mesh['clip'=8,'cap'=4] {'cap'}, use_global_device_ids=true, to_apply=%region_9.0 | all-reduce | flops 768 | bytes 6144 | tf_op jit(solution)/shard_map/psum | solution.py:46
  143.1 5.3 %convolution_bitcast_fusion = f32[1,1,1536]{2,1,0:T(1,128)S(1)} fusion(f32[768,1]{0,1:T(1,128)S(1)} %reshape.31, f32[768,1536]{1,0:T(8,128)} %get-tuple-element.7, f32[768]{0:T(1024)S(1)} %get-tuple-element.4), kind=kOutput, calls=%fused_computation.7 | convolution fusion | flops 16515072 | bytes 4730880 | tf_op jit(solution)/shard_map/dot_general | solution.py:42
  148.4 9.3 %all-gather.5 = f32[8,1,1536]{2,1,0:T(1,128)S(1)} all-gather(f32[1,1,1536]{2,1,0:T(1,128)S(1)} %convolution_bitcast_fusion), channel_id=4, replica_groups=mesh['clip'=8,'cap'=4] {'clip'}, dimensions={0}, use_global_device_ids=true | all-gather | bytes 55296 | tf_op jit(solution)/shard_map/all_gather | solution.py:42
  157.8 6.9 %convolution_reduce_fusion = f32[768]{0:T(1024)S(1)} fusion(f32[1536,1]{0,1:T(1,128)S(1)} %reshape.33, f32[768,1536]{1,0:T(8,128)} %get-tuple-element.7, f32[768]{0:T(1024)S(1)} %get-tuple-element.4), kind=kOutput, calls=%fused_computation.11 | convolution fusion | flops 16515072 | bytes 4730880 | tf_op jit(solution)/shard_map/dot_general | solution.py:46
  164.8 3.2 %fusion = f32[768]{0:T(1024)S(1)} fusion(f32[768,1536]{1,0:T(8,128)} %get-tuple-element.9, f32[768]{0:T(1024)S(1)} %get-tuple-element.5), kind=kLoop, calls=%fused_computation.5 | loop fusion | flops 3538176 | bytes 4724736 | tf_op jit(solution)/shard_map/reduce_sum | solution.py:36
  168.0 8.5 %all-reduce = (f32[768]{0:T(1024)S(1)}, f32[768]{0:T(1024)S(1)}) all-reduce(f32[768]{0:T(1024)S(1)} %convolution_reduce_fusion, f32[768]{0:T(1024)S(1)} %fusion), channel_id=1, replica_groups=mesh['clip'=8,'cap'=4] {'cap'}, use_global_device_ids=true, to_apply=%region_11.0 | all-reduce | flops 1536 | bytes 12288 | tf_op jit(solution)/shard_map/psum | solution.py:46
  176.5 0.0 copy-start
  176.6 4.9 %subtract_convert_fusion = bf16[768,1536]{1,0:T(8,128)(2,1)S(1)} fusion(f32[768,1536]{1,0:T(8,128)} %get-tuple-element.9, f32[1536]{0:T(1024)S(1)} %broadcast_divide_fusion, f32[768]{0:T(1024)S(1)} %broadcast_divide_fusion.5, f32[768]{0:T(1024)S(1)} %get-tuple-element.3, f32[768]{0:T(1024)S(1)} %get-tuple-element.5, f32[768]{0:T(1024)S(1)} %get-tuple-element.4, ...), kind=kLoop, calls=%fused_computation | loop fusion | flops 10616832 | bytes 11814912 | tf_op jit(solution)/shard_map/convert_element_type | solution.py:50
  181.5 0.0 copy-done
  181.5 2.5 convolution_multiply_fusion.1
  184.0 0.0 reduce-scatter.3.cloned.1.call-update
  184.1 0.0 reduce-scatter.5.cloned.1.call-start
  184.1 3.1 %convolution_multiply_fusion = f32[1536,512]{1,0:T(8,128)} fusion(bf16[768,1536]{1,0:T(8,128)(2,1)S(1)} %subtract_convert_fusion, bf16[768,512]{1,0:T(8,128)(2,1)S(1)} %all_gather.30), kind=kOutput, calls=%fused_computation.6 | convolution fusion | flops 1208745984 | bytes 6291456 | tf_op jit(solution)/shard_map/dot_general | solution.py:16
  187.2 0.0 reduce-scatter.5.cloned.1.call-update
  187.2 31.1 %reduce-scatter.3.cloned.1.call-done = f32[192,512]{1,0:T(8,128)} async-done(((f32[768,512]{1,0:T(8,128)}), f32[192,512]{1,0:T(8,128)}) %reduce-scatter.3.cloned.1.call-update) | async-done | bytes 393232 | tf_op jit(solution)/shard_map/reduce_scatter | solution.py:51
  218.3 48.7 %reduce-scatter.5.cloned.1.call-done = f32[192,512]{1,0:T(8,128)} async-done(((f32[1536,512]{1,0:T(8,128)}), f32[192,512]{1,0:T(8,128)}) %reduce-scatter.5.cloned.1.call-update) | async-done | bytes 393232 | tf_op jit(solution)/shard_map/reduce_scatter | solution.py:57
  (14 shorter events, 0.2 us)
Async XLA Ops:
  7.2 41.0 %all-gather.11.cloned.1.call-start = ((), (), s32[]{:S(2)}) async-start(), calls=%async_computation.3 | async-start | bytes 1769472 | tf_op jit(solution)/shard_map/all_gather | solution.py:27
  7.9 57.8 %all-gather.9.cloned.1.call-start = ((), (), s32[]{:S(2)}) async-start(), calls=%async_computation.2 | async-start | bytes 1769472 | tf_op jit(solution)/shard_map/all_gather | solution.py:28
  8.6 209.7 %reduce-scatter.3.cloned.1.call-start = ((), (), s32[]{:S(2)}) async-start(), calls=%async_computation.4 | async-start | bytes 1966080 | tf_op jit(solution)/shard_map/reduce_scatter | solution.py:51
  176.5 5.0 %copy-start = (bf16[1536,512]{1,0:T(8,128)(2,1)S(1)}, bf16[1536,512]{1,0:T(8,128)(2,1)}, u32[]{:S(2)}) copy-start(bf16[1536,512]{1,0:T(8,128)(2,1)} %all-gather.9.cloned.1.call-done) | copy-start | bytes 4718596
  184.1 83.0 %reduce-scatter.5.cloned.1.call-start = ((), (), s32[]{:S(2)}) async-start(), calls=%async_computation.5 | async-start | bytes 3538944 | tf_op jit(solution)/shard_map/reduce_scatter | solution.py:57
Sparse Core Ops, SparseCore 0:
  9.8 28.2 all-gather.10
  40.1 25.5 all-gather.8
  184.2 34.1 reduce-scatter.2
  222.1 44.8 reduce-scatter.4
